TPU v7x, 32 devices: a whole 2x2x4 slice. The times are simulated.
32 devices in a mesh: loop: 16 (over z, x, core), team: 2 (over y).
Axes of the slice: x: 2, y: 2, z: 4, core: 2. Of those that a mesh axis runs over, the one named last changes fastest.
Arguments:
- blocks: bfloat16 [4096, 128, 128], P(('loop', 'team')), may hold values from -0.078125 to 0.078125
- probes: bfloat16 [32768, 128], P(('loop', 'team')), may hold values from -6 to 6
- row_count: int32 [64], P(('loop', 'team')), may hold values from 0 to 64, as said below
- column_of_slot: int32 [4096], P(('loop', 'team')), may hold values from 0 to 255, as said below
Outputs:
- sketch: float32 [8192, 128], P(('loop', 'team'))
Inputs may be any that keep to these rules, and one draw needn't show every extreme that they name: `row_count`: A device's block rows hold 128 stored blocks or fewer together, and some device holds exactly 128; each block row holds at most min(64, 128), some block row exactly that many, and some block row none. `column_of_slot`: A used slot of a device in loop position t holds a block column in the pieces of loop indices t, t-1, ..., t-3 (mod 16), piece p covering block columns p * 16 to p * 16 + 15; columns within one block row are distinct. Unused slots hold columns of the same range.
All inputs are finite; a program needn't handle non-finite values.
Results may differ from a plain program's by a relative error of at most 0.0003.
Values may be sent and summed in bfloat16 or wider, within the bound.
A program may use at most 64 MiB of HBM per device.

v0:
```python
import jax
import jax.numpy as jnp
from jax import lax
from jax.sharding import PartitionSpec as P

STOPS = 3


def shifted(value, axis, steps):
    count = lax.axis_size(axis)
    pairs = [(source, (source + steps) % count) for source in range(count)]
    return lax.ppermute(value, axis, pairs)


def reach_lower(source):
    gathered = [source]
    current = source
    for number in range(STOPS):
        current = shifted(current, "loop", 1)
        gathered.append(current)
    return jnp.stack(gathered, axis=0)


def local(blocks, probes, row_count, column_of_slot):
    slot_count = blocks.shape[0]
    blk = blocks.shape[1]
    rows_here = row_count.shape[0]
    width = probes.shape[1]
    loop_size = lax.axis_size("loop")
    here = lax.axis_index("loop")
    piece = lax.all_gather(probes, "team", axis=0, tiled=True)
    window = reach_lower(piece)
    per_piece = window.shape[1] // blk
    tile_set = window.reshape(window.shape[0] * per_piece, blk, width)
    piece_of = column_of_slot // per_piece
    stop = (here - piece_of) % loop_size
    where_tile = stop * per_piece + column_of_slot % per_piece
    tiles = tile_set[where_tile]
    ends = jnp.cumsum(row_count)
    slot_entries = jnp.arange(slot_count, dtype=jnp.int32)
    owner = jnp.sum((slot_entries[:, None] >= ends[None, :]).astype(jnp.int32), axis=1)
    results = []
    for row_number in range(rows_here):
        keep = (owner == row_number).astype(jnp.bfloat16)
        masked = tiles * keep[:, None, None]
        results.append(
            jnp.einsum("sij,sjk->ik", blocks, masked, preferred_element_type=jnp.float32)
        )
    return jnp.concatenate(results, axis=0)


def solution(mesh):
    return jax.shard_map(
        local,
        mesh=mesh,
        in_specs=(
            P(("loop", "team"), None, None),
            P(("loop", "team"), None),
            P(("loop", "team")),
            P(("loop", "team")),
        ),
        out_specs=P(("loop", "team"), None),
        check_vma=False,
    )
```

profile of v0, /device:TPU:0, one launch (start us, length us, event | category | flops | bytes accessed | tf_op | source)
XLA Modules:
  0.0 57.3 jit_solution(10120173575876244232)
XLA Ops:
  0.0 10.2 %all_gather.3 = bf16[2048,128]{1,0:T(8,128)(2,1)S(1)} all-gather(bf16[1024,128]{1,0:T(8,128)(2,1)} %param.5), channel_id=1, replica_groups=mesh['loop'=16,'team'=2] {'team'}, dimensions={0}, use_global_device_ids=true | all-gather | bytes 786432 | tf_op jit(solution)/shard_map/all_gather | solution.py:31
  10.2 0.0 collective-permute-start
  10.2 11.3 %collective-permute-done = bf16[2048,128]{1,0:T(8,128)(2,1)S(1)} collective-permute-done((bf16[2048,128]{1,0:T(8,128)(2,1)S(1)}, bf16[2048,128]{1,0:T(8,128)(2,1)S(1)}, u32[]{:S(2)}, u32[]{:S(2)}) %collective-permute-start) | collective-permute-done | bytes 524320 | tf_op jit(solution)/shard_map/ppermute | solution.py:12
  21.5 0.0 collective-permute-start.1
  21.5 11.3 %collective-permute-done.1 = bf16[2048,128]{1,0:T(8,128)(2,1)S(1)} collective-permute-done((bf16[2048,128]{1,0:T(8,128)(2,1)S(1)}, bf16[2048,128]{1,0:T(8,128)(2,1)S(1)}, u32[]{:S(2)}, u32[]{:S(2)}) %collective-permute-start.1) | collective-permute-done | bytes 524320 | tf_op jit(solution)/shard_map/ppermute | solution.py:12
  32.8 0.0 copy-start.1
  32.8 0.0 collective-permute-start.2
  32.8 0.7 %compare_select_fusion = s32[128]{0:T(128)S(1)} fusion(s32[128]{0:T(128)} %param.7, s32[]{:T(128)S(6)} %axis_index.15), kind=kLoop, calls=%fused_computation.12 | loop fusion | flops 4608 | bytes 1028 | tf_op jit(solution)/shard_map/select_n | solution.py:38
  33.5 0.8 %reduce-window.8 = s32[2,1]{0,1:T(1,128)S(1)} reduce-window(s32[2,1]{0,1:T(1,128)} %bitcast.22, s32[]{:T(128)} %constant.42.clone.1), window={size=2x1 pad=1_0x0_0}, to_apply=%region_0.1 | reduce-window | flops 2 | bytes 20 | tf_op jit(solution)/shard_map/reduce-window.3
  34.3 0.1 fusion.12
  34.4 9.7 %collective-permute-done.2 = bf16[2048,128]{1,0:T(8,128)(2,1)S(1)} collective-permute-done((bf16[2048,128]{1,0:T(8,128)(2,1)S(1)}, bf16[2048,128]{1,0:T(8,128)(2,1)S(1)}, u32[]{:S(2)}, u32[]{:S(2)}) %collective-permute-start.2) | collective-permute-done | bytes 524320 | tf_op jit(solution)/shard_map/ppermute | solution.py:12
  44.1 0.0 copy-start.2
  44.1 0.0 copy-done.1
  44.1 0.8 %copy-done.2 = bf16[2048,128]{1,0:T(8,128)(2,1)} copy-done((bf16[2048,128]{1,0:T(8,128)(2,1)}, bf16[2048,128]{1,0:T(8,128)(2,1)S(1)}, u32[]{:S(2)}) %copy-start.2) | copy-done | bytes 524312
  44.9 1.5 %pad_maximum_fusion = bf16[4,2048,128]{2,1,0:T(8,128)(2,1)S(1)} fusion(bf16[1,2048,128]{2,1,0:T(8,128)(2,1)} %bitcast.21, bf16[1,2048,128]{2,1,0:T(8,128)(2,1)} %bitcast.20, bf16[1,2048,128]{2,1,0:T(8,128)(2,1)S(1)} %bitcast.19, bf16[1,2048,128]{2,1,0:T(8,128)(2,1)S(1)} %bitcast.18), kind=kLoop, calls=%fused_computation.5 | loop fusion | flops 3145728 | bytes 4194304 | tf_op jit(solution)/shard_map/stack | solution.py:21
  46.4 3.0 %gather_fusion = bf16[128,128,128]{2,1,0:T(8,128)(2,1)} fusion(bf16[64,128,128]{2,1,0:T(8,128)(2,1)S(1)} %bitcast.17, s32[1024]{0:T(1024)S(1)} %pad_clamp_fusion), kind=kCustom, calls=%fused_computation | custom fusion | bytes 8389120 | tf_op jit(solution)/shard_map/gather | solution.py:38
  49.4 0.0 copy-start
  49.4 0.0 copy-start.3
  49.4 4.9 %fusion.6 = f32[128,128]{1,0:T(8,128)S(1)} fusion(bf16[128,128,128]{2,1,0:T(8,128)(2,1)} %param.4, bf16[128,128,128]{2,1,0:T(8,128)(2,1)} %gather_fusion, bf16[128]{0:T(256)(128)(2,1)S(1)} %get-tuple-element.5), kind=kOutput, calls=%fused_computation.8 | convolution fusion | flops 538968064 | bytes 8454400 | tf_op jit(solution)/shard_map/sij,sjk->ik/dot_general | solution.py:47
  54.3 0.0 copy-done
  54.3 1.0 %copy-done.3 = bf16[128,128,128]{2,1,0:T(8,128)(2,1)S(1)} copy-done((bf16[128,128,128]{2,1,0:T(8,128)(2,1)S(1)}, bf16[128,128,128]{2,1,0:T(8,128)(2,1)}, u32[]{:S(2)}) %copy-start.3) | copy-done | bytes 4194328
  55.3 1.3 %fusion.9 = f32[128,128]{1,0:T(8,128)S(1)} fusion(bf16[128,128,128]{2,1,0:T(8,128)(2,1)S(1)} %copy-done.3, bf16[128,128,128]{2,1,0:T(8,128)(2,1)S(1)} %copy-done, bf16[128]{0:T(256)(128)(2,1)S(1)} %get-tuple-element.6), kind=kOutput, calls=%fused_computation.9 | convolution fusion | flops 538968064 | bytes 8454400 | tf_op jit(solution)/shard_map/sij,sjk->ik/dot_general | solution.py:47
  56.6 0.7 %pad_maximum_fusion.1 = f32[256,128]{1,0:T(8,128)} fusion(f32[128,128]{1,0:T(8,128)S(1)} %fusion.9, f32[128,128]{1,0:T(8,128)S(1)} %fusion.6), kind=kLoop, calls=%fused_computation.10 | loop fusion | flops 32768 | bytes 262144 | tf_op jit(solution)/shard_map/concatenate | solution.py:49
  (2 shorter events, 0.0 us)
Async XLA Ops:
  10.2 11.3 %collective-permute-start = (bf16[2048,128]{1,0:T(8,128)(2,1)S(1)}, bf16[2048,128]{1,0:T(8,128)(2,1)S(1)}, u32[]{:S(2)}, u32[]{:S(2)}) collective-permute-start(bf16[2048,128]{1,0:T(8,128)(2,1)S(1)} %all_gather.3), channel_id=1, source_target_pairs={{0,2},{2,4},{4,6},{6,8},{8,10},{10,12},{12,14},{14,16},{16,18},{18... | collective-permute-start | bytes 1572872 | tf_op jit(solution)/shard_map/ppermute | solution.py:12
  21.5 11.3 %collective-permute-start.1 = (bf16[2048,128]{1,0:T(8,128)(2,1)S(1)}, bf16[2048,128]{1,0:T(8,128)(2,1)S(1)}, u32[]{:S(2)}, u32[]{:S(2)}) collective-permute-start(bf16[2048,128]{1,0:T(8,128)(2,1)S(1)} %collective-permute-done), channel_id=1, source_target_pairs={{0,2},{2,4},{4,6},{6,8},{8,10},{10,12},{12,14},{14,16},{16,18},{18... | collective-permute-start | bytes 1572872 | tf_op jit(solution)/shard_map/ppermute | solution.py:12
  32.8 11.3 %copy-start.1 = (bf16[2048,128]{1,0:T(8,128)(2,1)}, bf16[2048,128]{1,0:T(8,128)(2,1)S(1)}, u32[]{:S(2)}) copy-start(bf16[2048,128]{1,0:T(8,128)(2,1)S(1)} %collective-permute-done.1) | copy-start | bytes 1572868
  32.8 11.3 %collective-permute-start.2 = (bf16[2048,128]{1,0:T(8,128)(2,1)S(1)}, bf16[2048,128]{1,0:T(8,128)(2,1)S(1)}, u32[]{:S(2)}, u32[]{:S(2)}) collective-permute-start(bf16[2048,128]{1,0:T(8,128)(2,1)S(1)} %collective-permute-done.1), channel_id=1, source_target_pairs={{0,2},{2,4},{4,6},{6,8},{8,10},{10,12},{12,14},{14,16},{16,18},{18... | collective-permute-start | bytes 1572872 | tf_op jit(solution)/shard_map/ppermute | solution.py:12
  44.1 0.8 %copy-start.2 = (bf16[2048,128]{1,0:T(8,128)(2,1)}, bf16[2048,128]{1,0:T(8,128)(2,1)S(1)}, u32[]{:S(2)}) copy-start(bf16[2048,128]{1,0:T(8,128)(2,1)S(1)} %collective-permute-done.2) | copy-start | bytes 1572868
  49.4 4.9 %copy-start = (bf16[128,128,128]{2,1,0:T(8,128)(2,1)S(1)}, bf16[128,128,128]{2,1,0:T(8,128)(2,1)}, u32[]{:S(2)}) copy-start(bf16[128,128,128]{2,1,0:T(8,128)(2,1)} %gather_fusion) | copy-start | bytes 12582916
  49.4 5.9 %copy-start.3 = (bf16[128,128,128]{2,1,0:T(8,128)(2,1)S(1)}, bf16[128,128,128]{2,1,0:T(8,128)(2,1)}, u32[]{:S(2)}) copy-start(bf16[128,128,128]{2,1,0:T(8,128)(2,1)} %param.4) | copy-start | bytes 12582916
where the time goes:
time: 57.4 us; the launch traced here: 57.3 us
  waiting for transfers between devices  32.3 us (56%)
  blocking collectives  10.2 us (18%)
  matrix products  6.22 us (11%)
  local copies, waits for them, and re-layouts  4.81 us (8%)
  other arithmetic  3.75 us (7%)
    ppermute x3, waiting for transfers between devices, shifted(): return lax.ppermute(value, axis, pairs)  32.3 us
    all_gather x1, blocking collectives, local(): piece = lax.all_gather(probes, 'team', axis=0, tiled=True)  10.2 us
    dot_general x2, matrix products, local(): jnp.einsum('sij,sjk->ik', blocks, masked, preferred_element_type=jnp.floa...  6.22 us
    gather x1, local copies, waits for them, and re-layouts, local(): tiles = tile_set[where_tile]  3.02 us
    unnamed x8, local copies, waits for them, and re-layouts  1.79 us
    another operation x1, other arithmetic, reach_lower(): return jnp.stack(gathered, axis=0)  1.46 us
  transfers between devices with their start and end apart: 3, of which 3 were waited for; matrix products, arithmetic and copies ran while one was open for 3% of the time, Pallas kernels for 0%

commit v1 on v0

v1 whole, which is shorter than its diff:
```python
import functools

import jax
import jax.numpy as jnp
from jax import lax
from jax.experimental import pallas as pl
from jax.experimental.pallas import tpu as pltpu
from jax.sharding import PartitionSpec as P

STOPS = 4
LANES = 128


def kernel(geo, counts_ref, cols_ref, blocks_ref, probes_ref, out_ref,
           blk, win, inv_v, inv_s, recv, send, loc):
    loop_n, team_n, chunks, early, rows_here, slots, edge, tps = geo
    chunk = tps * edge // chunks
    per_piece = team_n * tps
    span = STOPS * per_piece
    t = lax.axis_index("loop")
    m = lax.axis_index("team")
    core = lax.rem(t, 2)

    def at(dt, dm):
        return {"loop": lax.rem(t + dt + loop_n, loop_n), "team": lax.rem(m + dm + team_n, team_n)}

    blk_copy = pltpu.make_async_copy(blocks_ref, blk.at[pl.ds(0, slots)], loc.at[0])
    blk_copy.start()
    own_copy = pltpu.make_async_copy(probes_ref, win.at[0, 0], loc.at[1])
    own_copy.start()

    barrier = pltpu.get_barrier_semaphore()
    peers = [(0, d) for d in range(1, team_n)]
    peers += [(1 - 2 * core, 0), (2, 0), (-2, 0), (6 * core - 3, 0)]
    for dt, dm in peers:
        pl.semaphore_signal(barrier, inc=1, device_id=at(dt, dm), device_id_type=pl.DeviceIdType.MESH)
    pl.semaphore_wait(barrier, len(peers))

    sent = []

    def rows(c):
        return pl.ds(c * chunk, chunk)

    def push(src, k, d, c, where, only=None):
        number = len(sent)
        copy = pltpu.make_async_remote_copy(
            src_ref=src, dst_ref=win.at[k, d, rows(c)],
            send_sem=send.at[number], recv_sem=recv.at[k, d, c],
            device_id=where, device_id_type=pl.DeviceIdType.MESH)
        sent.append((copy, only))
        if only is None:
            copy.start()
        else:
            pl.when(only)(copy.start)

    def arrive(k, d, c):
        pltpu.make_async_copy(win.at[k, d, rows(c)], win.at[k, d, rows(c)], recv.at[k, d, c]).wait()

    partner = at(1 - 2 * core, 0)
    across = at(1 + 2 * core, 0)
    lower = core == 0

    for c in range(chunks):
        own = probes_ref.at[rows(c)]
        for d in range(1, team_n):
            push(own, 0, d, c, at(0, d))
        push(own, 2, 0, c, at(2, 0))
        push(own, 1 + 2 * core, 0, c, across)

    place = lax.broadcasted_iota(jnp.int32, inv_v.shape, 0) * LANES
    place = place + lax.broadcasted_iota(jnp.int32, inv_v.shape, 1)

    def enter(s, table):
        col = cols_ref[s]
        stop = lax.rem(t - lax.div(col, per_piece) + loop_n, loop_n)
        within = lax.rem(col, per_piece)
        member = lax.rem(m - lax.div(within, tps) + team_n, team_n)
        key = (stop * team_n + member) * tps + lax.rem(within, tps)
        end = jnp.int32(0)
        for r in range(rows_here):
            end = end + counts_ref[r]
            key = key + jnp.where(s >= end, span, 0)
        return jnp.where((place == key) & (s < end), s, table)

    inv_v[...] = lax.fori_loop(0, slots, enter, jnp.full(inv_v.shape, slots, jnp.int32), unroll=4)
    inv_copy = pltpu.make_async_copy(inv_v, inv_s, loc.at[2])
    inv_copy.start()
    blk[slots] = jnp.zeros(blk.shape[1:], blk.dtype)
    out_ref[...] = jnp.zeros_like(out_ref)

    step = 2 if tps % 2 == 0 else 1

    def compute(k, d):
        base = (k * team_n + d) * tps
        total = None
        for j in range(0, tps, step):
            left = []
            for r in range(rows_here):
                pair = []
                for i in range(step):
                    key = r * span + base + j + i
                    pair.append(blk[inv_s[key // LANES, key % LANES]])
                left.append(jnp.concatenate(pair, axis=1))
            part = jnp.dot(jnp.concatenate(left, axis=0), win[k, d, pl.ds(j * edge, step * edge)],
                           preferred_element_type=jnp.float32)
            total = part if total is None else total + part
        out_ref[...] += total

    for c in range(chunks):
        for d in range(1, team_n):
            arrive(0, d, c)
            got = win.at[0, d, rows(c)]
            if c < early:
                push(got, 2, d, c, at(2, 0))
                push(got, 1 + 2 * core, d, c, across)
            else:
                push(got, 1, d, c, partner, lower)
        arrive(2, 0, c)
        got = win.at[2, 0, rows(c)]
        if c >= early:
            for d in range(1, team_n):
                push(got, 2, d, c, at(0, d))
        push(got, 3 - 2 * core, 0, c, partner)

    inv_copy.wait()
    blk_copy.wait()
    own_copy.wait()
    for d in range(team_n):
        compute(0, d)
    compute(2, 0)

    for c in range(chunks):
        arrive(3, 0, c)
        if c >= early:
            for d in range(1, team_n):
                push(win.at[3, 0, rows(c)], 3, d, c, at(0, d), lower)
        for d in range(1, team_n):
            arrive(2, d, c)
            push(win.at[2, d, rows(c)], 3 - 2 * core, d, c, partner)

    compute(3, 0)
    for d in range(1, team_n):
        compute(2, d)
    for d in range(team_n):
        for c in range(chunks):
            arrive(1, d, c)
        compute(1, d)
    for d in range(1, team_n):
        for c in range(chunks):
            arrive(3, d, c)
        compute(3, d)

    for copy, only in sent:
        if only is None:
            copy.wait_send()
        else:
            pl.when(only)(copy.wait_send)


def sends(team_n, chunks, early):
    late = chunks - early
    mates = team_n - 1
    return chunks * (mates + 2) + mates * (2 * early + late) + late * mates + chunks + late * mates + mates * chunks


def local(loop_n, team_n, blocks, probes, row_count, column_of_slot):
    slots, edge, _ = blocks.shape
    width = probes.shape[1]
    tps = probes.shape[0] // edge
    rows_here = row_count.shape[0]
    chunks = min(4, tps)
    early = chunks // 2
    geo = (loop_n, team_n, chunks, early, rows_here, slots, edge, tps)
    entries = rows_here * STOPS * team_n * tps
    table = (-(-entries // (8 * LANES)) * 8, LANES)
    return pl.pallas_call(
        functools.partial(kernel, geo),
        out_shape=jax.ShapeDtypeStruct((rows_here * edge, width), jnp.float32),
        in_specs=[
            pl.BlockSpec(memory_space=pltpu.SMEM),
            pl.BlockSpec(memory_space=pltpu.SMEM),
            pl.BlockSpec(memory_space=pltpu.HBM),
            pl.BlockSpec(memory_space=pltpu.HBM),
        ],
        out_specs=pl.BlockSpec(memory_space=pltpu.VMEM),
        scratch_shapes=[
            pltpu.VMEM((slots + 1, edge, edge), blocks.dtype),
            pltpu.VMEM((STOPS, team_n, tps * edge, width), probes.dtype),
            pltpu.VMEM(table, jnp.int32),
            pltpu.SMEM(table, jnp.int32),
            pltpu.SemaphoreType.DMA((STOPS, team_n, chunks)),
            pltpu.SemaphoreType.DMA((sends(team_n, chunks, early),)),
            pltpu.SemaphoreType.DMA((3,)),
        ],
        compiler_params=pltpu.CompilerParams(
            collective_id=0, has_side_effects=True, vmem_limit_bytes=60 * 1024 * 1024),
    )(row_count, column_of_slot, blocks, probes)


def solution(mesh):
    spec = ("loop", "team")
    return jax.shard_map(
        functools.partial(local, mesh.shape["loop"], mesh.shape["team"]),
        mesh=mesh,
        in_specs=(P(spec, None, None), P(spec, None), P(spec), P(spec)),
        out_specs=P(spec, None),
        check_vma=False,
    )
```

time: 57.4 us -> 25.3 us (0.44)
  waiting for transfers between devices: 32.3 us -> 0 us
  Pallas kernels: 0 us -> 23.5 us
  blocking collectives: 10.2 us -> 0 us
  matrix products: 6.22 us -> 0 us
  other arithmetic: 3.75 us -> 0 us
  local copies, waits for them, and re-layouts: 4.81 us -> 1.57 us
    ppermute x3 -> x0, waiting for transfers between devices: 32.3 us -> none  [shifted(): return lax.ppermute(value, axis, pairs)]
    pallas_call x0 -> x1, Pallas kernels: none -> 23.5 us  [local(): pl.pallas_call(functools.partial(kernel, geo), out_shape=jax.ShapeDtypeSt...]
    all_gather x1 -> x0, blocking collectives: 10.2 us -> none  [local(): piece = lax.all_gather(probes, 'team', axis=0, tiled=True)]
    dot_general x2 -> x0, matrix products: 6.22 us -> none  [local(): jnp.einsum('sij,sjk->ik', blocks, masked, preferred_element_type=jnp.floa...]
    gather x1 -> x0, local copies, waits for them, and re-layouts: 3.02 us -> none  [local(): tiles = tile_set[where_tile]]
    another operation x2 -> x0, other arithmetic: 2.28 us -> none  [the longest x1 1.46 us: reach_lower(): return jnp.stack(gathered, axis=0)]
    select_n x1 -> x0, other arithmetic: 0.7 us -> none  [local(): tiles = tile_set[where_tile]]
    concatenate x1 -> x0, other arithmetic: 0.67 us -> none  [local(): return jnp.concatenate(results, axis=0)]
  transfers between devices with their start and end apart: 3 -> 0, of which waited for: 3 -> 0; matrix products, arithmetic and copies ran while one was open for 3% -> 0% of each run, Pallas kernels for 0% -> 0%
where the time goes in v1:
time: 25.3 us; the launch traced here: 25.1 us
  Pallas kernels  23.5 us (93%)
  local copies, waits for them, and re-layouts  1.57 us (6%)
    pallas_call x1, Pallas kernels, local(): pl.pallas_call(functools.partial(kernel, geo), out_shape=jax.ShapeDtypeSt...  23.5 us
    unnamed x1, local copies, waits for them, and re-layouts  1.57 us

profile of v1, /device:TPU:0, one launch (start us, length us, event | category | flops | bytes accessed | tf_op | source)
XLA Modules:
  0.0 25.1 jit_solution(8611689187679183516)
XLA Ops:
  0.0 23.5 %shard_map.46 = f32[256,128]{1,0:T(8,128)} custom-call(s32[2]{0:T(128)} %counts_ref.1, s32[128]{0:T(128)} %cols_ref.1, bf16[128,128,128]{2,1,0:T(8,128)(2,1)} %blocks_ref.1, bf16[1024,128]{1,0:T(8,128)(2,1)} %probes_ref.1), custom_call_target="tpu_custom_call" | custom-call | tf_op jit(solution)/shard_map/pallas_call | solution.py:176
  23.5 1.6 %copy.6 = f32[256,128]{1,0:T(8,128)} copy(f32[256,128]{1,0:T(8,128)} %shard_map.46) | data formatting | bytes 262144

commit v2 on v1

v2 whole, which is shorter than its diff:
```python
import functools

import jax
import jax.numpy as jnp
from jax import lax
from jax.experimental import pallas as pl
from jax.experimental.pallas import tpu as pltpu
from jax.sharding import PartitionSpec as P

STOPS = 4
LANES = 128


def kernel(geo, counts_hbm, cols_hbm, blocks_ref, probes_ref, out_ref,
           blk, win, counts_ref, cols_ref, inv_v, inv_s, recv, send, loc):
    loop_n, team_n, chunks, early, early_wrap, rows_here, slots, edge, tps = geo
    chunk = tps * edge // chunks
    per_piece = team_n * tps
    span = STOPS * per_piece
    t = lax.axis_index("loop")
    m = lax.axis_index("team")
    core = lax.rem(t, 2)
    odd = lax.rem(lax.div(t, 2), 2)
    lower = core == 0
    passes = lower & (odd == 1)
    direct = (core == 0) | (odd == 0)

    def at(dt, dm):
        return {"loop": lax.rem(t + dt + loop_n, loop_n), "team": lax.rem(m + dm + team_n, team_n)}

    copies = [
        pltpu.make_async_copy(counts_hbm, counts_ref, loc.at[0]),
        pltpu.make_async_copy(cols_hbm, cols_ref, loc.at[1]),
        pltpu.make_async_copy(probes_ref, win.at[0, 0], loc.at[2]),
        pltpu.make_async_copy(blocks_ref, blk.at[pl.ds(0, slots)], loc.at[3]),
    ]
    for copy in copies:
        copy.start()

    barrier = pltpu.get_barrier_semaphore()

    def greet(dt, dm):
        pl.semaphore_signal(barrier, inc=1, device_id=at(dt, dm), device_id_type=pl.DeviceIdType.MESH)

    pl.when(lower)(lambda: greet(-3, 0))
    greet(jnp.where((core == 1) & (odd == 0), 1, -2), 0)
    for d in range(1, team_n):
        greet(0, d)
    greet(1 - 2 * core, 0)

    copies[0].wait()
    copies[1].wait()
    place = lax.broadcasted_iota(jnp.int32, inv_v.shape, 0) * LANES
    place = place + lax.broadcasted_iota(jnp.int32, inv_v.shape, 1)

    def enter(s, table):
        col = cols_ref[s]
        stop = lax.rem(t - lax.div(col, per_piece) + loop_n, loop_n)
        within = lax.rem(col, per_piece)
        member = lax.rem(m - lax.div(within, tps) + team_n, team_n)
        key = (stop * team_n + member) * tps + lax.rem(within, tps)
        end = jnp.int32(0)
        for r in range(rows_here):
            end = end + counts_ref[r]
            key = key + jnp.where(s >= end, span, 0)
        return jnp.where((place == key) & (s < end), s, table)

    inv_v[...] = lax.fori_loop(0, slots, enter, jnp.full(inv_v.shape, slots, jnp.int32), unroll=8)
    inv_copy = pltpu.make_async_copy(inv_v, inv_s, loc.at[4])
    inv_copy.start()
    blk[slots] = jnp.zeros(blk.shape[1:], blk.dtype)

    pl.semaphore_wait(barrier, team_n + 1 + jnp.where(core == odd, 0, 1))

    sent = []

    def rows(c):
        return pl.ds(c * chunk, chunk)

    def push(src, k, d, c, where, only=None):
        copy = pltpu.make_async_remote_copy(
            src_ref=src, dst_ref=win.at[k, d, rows(c)],
            send_sem=send.at[len(sent)], recv_sem=recv.at[k, d, c],
            device_id=where, device_id_type=pl.DeviceIdType.MESH)
        sent.append((copy, only))
        if only is None:
            copy.start()
        else:
            pl.when(only)(copy.start)

    def arrive(k, d, c):
        pltpu.make_async_copy(win.at[k, d, rows(c)], win.at[k, d, rows(c)], recv.at[k, d, c]).wait()

    def first(c, limit):
        return limit > c

    partner = at(1 - 2 * core, 0)
    ahead = at(2, 0)
    across = at(1 + 2 * core, 0)
    back = at(-1, 0)
    out2 = jnp.where(t + 2 >= loop_n, early_wrap, early)
    out3 = jnp.where(t + 3 >= loop_n, early_wrap, early)
    in2 = jnp.where(t < 2, early_wrap, early)
    in3 = jnp.where(t < 3, early_wrap, early)

    for c in range(chunks):
        own = probes_ref.at[rows(c)]
        for d in range(1, team_n):
            push(own, 0, d, c, at(0, d))
        push(own, 1 + 2 * core, 0, c, across)
        push(own, 2, 0, c, ahead, direct)

    inv_copy.wait()
    copies[2].wait()
    copies[3].wait()
    step = 2 if tps % 2 == 0 else 1

    def compute(k, d):
        base = (k * team_n + d) * tps
        total = None
        for j in range(0, tps, step):
            left = []
            for r in range(rows_here):
                pair = []
                for i in range(step):
                    key = r * span + base + j + i
                    pair.append(blk[inv_s[key // LANES, key % LANES]])
                left.append(jnp.concatenate(pair, axis=1))
            part = jnp.dot(jnp.concatenate(left, axis=0), win[k, d, pl.ds(j * edge, step * edge)],
                           preferred_element_type=jnp.float32)
            total = part if total is None else total + part
        if k == 0 and d == 0:
            out_ref[...] = total
        else:
            out_ref[...] += total

    compute(0, 0)
    for c in range(chunks):
        for d in range(1, team_n):
            arrive(0, d, c)
            got = win.at[0, d, rows(c)]
            push(got, 2, d, c, ahead, direct & first(c, out2))
            push(got, 1 + 2 * core, d, c, across, lower | first(c, out3))
    for d in range(1, team_n):
        compute(0, d)

    for c in range(chunks):
        @pl.when(lower)
        def _():
            arrive(3, 0, c)
        got = win.at[3, 0, rows(c)]
        push(got, 2, 0, c, back, passes)
        for d in range(1, team_n):
            push(got, 3, d, c, at(0, d), lower & ~first(c, in3))
        arrive(2, 0, c)
        got = win.at[2, 0, rows(c)]
        for d in range(1, team_n):
            push(got, 2, d, c, at(0, d), ~first(c, in2))
        push(got, 3 - 2 * core, 0, c, partner)
    compute(2, 0)

    for c in range(chunks):
        for d in range(1, team_n):
            @pl.when(lower)
            def _():
                arrive(3, d, c)
            push(win.at[3, d, rows(c)], 2, d, c, back, passes & first(c, in3))
            arrive(2, d, c)
            push(win.at[2, d, rows(c)], 3 - 2 * core, d, c, partner)

    for d in range(1, team_n):
        compute(2, d)
    for d in range(team_n):
        for c in range(chunks):
            arrive(1, d, c)
        compute(1, d)
    for d in range(team_n):
        @pl.when(core == 1)
        def _():
            for c in range(chunks):
                arrive(3, d, c)
        compute(3, d)

    for copy, only in sent:
        if only is None:
            copy.wait_send()
        else:
            pl.when(only)(copy.wait_send)


def sends(team_n, chunks):
    mates = team_n - 1
    return chunks * (mates + 2 + 2 * mates + 1 + mates + mates + 1 + 2 * mates)


def local(loop_n, team_n, blocks, probes, row_count, column_of_slot):
    slots, edge, _ = blocks.shape
    width = probes.shape[1]
    tps = probes.shape[0] // edge
    rows_here = row_count.shape[0]
    chunks = min(8, tps)
    early = chunks * 5 // 8
    early_wrap = chunks // 4
    geo = (loop_n, team_n, chunks, early, early_wrap, rows_here, slots, edge, tps)
    entries = rows_here * STOPS * team_n * tps
    table = (-(-entries // (8 * LANES)) * 8, LANES)
    return pl.pallas_call(
        functools.partial(kernel, geo),
        out_shape=jax.ShapeDtypeStruct((rows_here * edge, width), jnp.float32),
        in_specs=[
            pl.BlockSpec(memory_space=pltpu.HBM),
            pl.BlockSpec(memory_space=pltpu.HBM),
            pl.BlockSpec(memory_space=pltpu.HBM),
            pl.BlockSpec(memory_space=pltpu.HBM),
        ],
        out_specs=pl.BlockSpec(memory_space=pltpu.VMEM),
        scratch_shapes=[
            pltpu.VMEM((slots + 1, edge, edge), blocks.dtype),
            pltpu.VMEM((STOPS, team_n, tps * edge, width), probes.dtype),
            pltpu.SMEM(row_count.shape, jnp.int32),
            pltpu.SMEM(column_of_slot.shape, jnp.int32),
            pltpu.VMEM(table, jnp.int32),
            pltpu.SMEM(table, jnp.int32),
            pltpu.SemaphoreType.DMA((STOPS, team_n, chunks)),
            pltpu.SemaphoreType.DMA((sends(team_n, chunks),)),
            pltpu.SemaphoreType.DMA((5,)),
        ],
        compiler_params=pltpu.CompilerParams(
            collective_id=0, has_side_effects=True, vmem_limit_bytes=60 * 1024 * 1024),
    )(row_count, column_of_slot, blocks, probes)


def solution(mesh):
    spec = ("loop", "team")
    return jax.shard_map(
        functools.partial(local, mesh.shape["loop"], mesh.shape["team"]),
        mesh=mesh,
        in_specs=(P(spec, None, None), P(spec, None), P(spec), P(spec)),
        out_specs=P(spec, None),
        check_vma=False,
    )
```

time: 25.3 us -> 26.9 us (1.063)
  Pallas kernels: 23.5 us -> 25.1 us
    pallas_call x1, Pallas kernels: 23.5 us -> 25.1 us  [local(): pl.pallas_call(functools.partial(kernel, geo), out_shape=jax.ShapeDtypeSt...]
where the time goes in v2:
time: 26.9 us; the launch traced here: 26.7 us
  Pallas kernels  25.1 us (93%)
  local copies, waits for them, and re-layouts  1.57 us (6%)
    pallas_call x1, Pallas kernels, local(): pl.pallas_call(functools.partial(kernel, geo), out_shape=jax.ShapeDtypeSt...  25.1 us
    unnamed x1, local copies, waits for them, and re-layouts  1.57 us

profile of v2, /device:TPU:0, one launch (start us, length us, event | category | flops | bytes accessed | tf_op | source)
XLA Modules:
  0.0 26.7 jit_solution(8730448829341104863)
XLA Ops:
  0.0 25.1 %shard_map.46 = f32[256,128]{1,0:T(8,128)} custom-call(s32[2]{0:T(128)} %counts_hbm.1, s32[128]{0:T(128)} %cols_hbm.1, bf16[128,128,128]{2,1,0:T(8,128)(2,1)} %blocks_ref.1, bf16[1024,128]{1,0:T(8,128)(2,1)} %probes_ref.1), custom_call_target="tpu_custom_call" | custom-call | tf_op jit(solution)/shard_map/pallas_call | solution.py:207
  25.1 1.6 %copy.6 = f32[256,128]{1,0:T(8,128)} copy(f32[256,128]{1,0:T(8,128)} %shard_map.46) | data formatting | bytes 262144

commit v3 on v2

v3 whole, which is shorter than its diff:
```python
import functools

import jax
import jax.numpy as jnp
from jax import lax
from jax.experimental import pallas as pl
from jax.experimental.pallas import tpu as pltpu
from jax.sharding import PartitionSpec as P

STOPS = 4
LANES = 128


def div(x, n):
    return lax.shift_right_logical(x, n.bit_length() - 1) if n & (n - 1) == 0 else lax.div(x, n)


def rem(x, n):
    return x & (n - 1) if n & (n - 1) == 0 else lax.rem(x, n)


def kernel(geo, counts_hbm, cols_hbm, blocks_ref, probes_ref, out_ref,
           blk, win, counts_ref, cols_ref, inv_v, inv_s, recv, send, loc):
    loop_n, team_n, chunks, early, rows_here, slots, edge, tps = geo
    chunk = tps * edge // chunks
    per_piece = team_n * tps
    span = STOPS * per_piece
    t = lax.axis_index("loop")
    m = lax.axis_index("team")
    core = lax.rem(t, 2)
    odd = lax.rem(lax.div(t, 2), 2)
    lower = core == 0

    def at(dt, dm):
        return {"loop": lax.rem(t + dt + loop_n, loop_n), "team": lax.rem(m + dm + team_n, team_n)}

    copies = [
        pltpu.make_async_copy(counts_hbm, counts_ref, loc.at[0]),
        pltpu.make_async_copy(cols_hbm, cols_ref, loc.at[1]),
        pltpu.make_async_copy(probes_ref, win.at[0, 0], loc.at[2]),
        pltpu.make_async_copy(blocks_ref, blk.at[pl.ds(0, slots)], loc.at[3]),
    ]
    for copy in copies:
        copy.start()

    barrier = pltpu.get_barrier_semaphore()

    def greet(dt, dm):
        pl.semaphore_signal(barrier, inc=1, device_id=at(dt, dm), device_id_type=pl.DeviceIdType.MESH)

    pl.when(lower)(lambda: greet(-3, 0))
    greet(-2, 0)
    for d in range(1, team_n):
        greet(0, d)
    greet(1 - 2 * core, 0)

    copies[0].wait()
    copies[1].wait()
    col = cols_ref[...]
    within = rem(col, per_piece)
    stop = rem(t - div(col, per_piece) + loop_n, loop_n)
    member = rem(m - div(within, tps) + team_n, team_n)
    key = (stop * team_n + member) * tps + rem(within, tps)
    number = lax.broadcasted_iota(jnp.int32, key.shape, 1)
    end = jnp.int32(0)
    for r in range(rows_here):
        end = end + counts_ref[r]
        key = key + jnp.where(number >= end, span, 0)
    key = jnp.where(number < end, key, -1)
    entries = inv_v.shape[1]
    keys = jnp.broadcast_to(key, (LANES, slots)).T[:, :1]
    hit = keys == lax.broadcasted_iota(jnp.int32, (slots, entries), 1)
    owner = jnp.where(hit, lax.broadcasted_iota(jnp.int32, (slots, entries), 0), slots)
    inv_v[...] = jnp.min(owner, axis=0, keepdims=True)
    inv_copy = pltpu.make_async_copy(inv_v, inv_s, loc.at[4])
    inv_copy.start()
    blk[slots] = jnp.zeros(blk.shape[1:], blk.dtype)

    pl.semaphore_wait(barrier, team_n + 1 + core)

    sent = []

    def rows(c):
        return pl.ds(c * chunk, chunk)

    def push(src, k, d, c, where, only=None):
        copy = pltpu.make_async_remote_copy(
            src_ref=src, dst_ref=win.at[k, d, rows(c)],
            send_sem=send.at[len(sent)], recv_sem=recv.at[k, d, c],
            device_id=where, device_id_type=pl.DeviceIdType.MESH)
        sent.append((copy, only))
        if only is None:
            copy.start()
        else:
            pl.when(only)(copy.start)

    def arrive(k, d, c):
        pltpu.make_async_copy(win.at[k, d, rows(c)], win.at[k, d, rows(c)], recv.at[k, d, c]).wait()

    def first(c, limit):
        return limit > c

    partner = at(1 - 2 * core, 0)
    ahead = at(2, 0)
    across = at(1 + 2 * core, 0)
    even2, odd2, even3, odd3 = early
    out2 = jnp.where(odd == 1, odd2, even2)
    out3 = jnp.where(odd == 1, odd3, even3)
    in2 = jnp.where(odd == 1, even2, odd2)
    in3 = out3

    for c in range(chunks):
        own = probes_ref.at[rows(c)]
        push(own, 2, 0, c, ahead)
        push(own, 1 + 2 * core, 0, c, across)
        for d in range(1, team_n):
            push(own, 0, d, c, at(0, d))

    inv_copy.wait()
    copies[2].wait()
    copies[3].wait()
    step = 2 if tps % 2 == 0 else 1

    def compute(k, d):
        base = (k * team_n + d) * tps
        total = None
        for j in range(0, tps, step):
            left = []
            for r in range(rows_here):
                pair = []
                for i in range(step):
                    key = r * span + base + j + i
                    pair.append(blk[inv_s[0, key]])
                left.append(jnp.concatenate(pair, axis=1))
            part = jnp.dot(jnp.concatenate(left, axis=0), win[k, d, pl.ds(j * edge, step * edge)],
                           preferred_element_type=jnp.float32)
            total = part if total is None else total + part
        if k == 0 and d == 0:
            out_ref[...] = total
        else:
            out_ref[...] += total

    compute(0, 0)
    for c in range(chunks):
        for d in range(1, team_n):
            arrive(0, d, c)
            got = win.at[0, d, rows(c)]
            push(got, 2, d, c, ahead, first(c, out2))
            push(got, 1 + 2 * core, d, c, across, lower | first(c, out3))

    for c in range(chunks):
        arrive(2, 0, c)
        got = win.at[2, 0, rows(c)]
        for d in range(1, team_n):
            push(got, 2, d, c, at(0, d), ~first(c, in2))
        push(got, 3 - 2 * core, 0, c, partner)

        @pl.when(lower)
        def _():
            arrive(3, 0, c)
        for d in range(1, team_n):
            push(win.at[3, 0, rows(c)], 3, d, c, at(0, d), lower & ~first(c, in3))

    for d in range(1, team_n):
        compute(0, d)
    compute(2, 0)
    for c in range(chunks):
        arrive(1, 0, c)
    compute(1, 0)

    @pl.when(core == 1)
    def _():
        for c in range(chunks):
            arrive(3, 0, c)
    compute(3, 0)

    for c in range(chunks):
        for d in range(1, team_n):
            arrive(2, d, c)
            push(win.at[2, d, rows(c)], 3 - 2 * core, d, c, partner)

    for k in (2, 1, 3):
        for d in range(1, team_n):
            if k != 2:
                for c in range(chunks):
                    arrive(k, d, c)
            compute(k, d)

    for copy, only in sent:
        if only is None:
            copy.wait_send()
        else:
            pl.when(only)(copy.wait_send)


def sends(team_n, chunks):
    mates = team_n - 1
    return chunks * (2 + mates + 2 * mates + mates + 1 + mates + mates)


def local(loop_n, team_n, blocks, probes, row_count, column_of_slot):
    slots, edge, _ = blocks.shape
    width = probes.shape[1]
    tps = probes.shape[0] // edge
    rows_here = row_count.shape[0]
    chunks = min(4, tps)
    early = (chunks // 2, chunks // 4, chunks, chunks // 4)
    geo = (loop_n, team_n, chunks, early, rows_here, slots, edge, tps)
    entries = rows_here * STOPS * team_n * tps
    table = (1, -(-entries // LANES) * LANES)
    return pl.pallas_call(
        functools.partial(kernel, geo),
        out_shape=jax.ShapeDtypeStruct((rows_here * edge, width), jnp.float32),
        in_specs=[
            pl.BlockSpec(memory_space=pltpu.HBM),
            pl.BlockSpec(memory_space=pltpu.HBM),
            pl.BlockSpec(memory_space=pltpu.HBM),
            pl.BlockSpec(memory_space=pltpu.HBM),
        ],
        out_specs=pl.BlockSpec(memory_space=pltpu.VMEM),
        scratch_shapes=[
            pltpu.VMEM((slots + 1, edge, edge), blocks.dtype),
            pltpu.VMEM((STOPS, team_n, tps * edge, width), probes.dtype),
            pltpu.SMEM(row_count.shape, jnp.int32),
            pltpu.VMEM((1, slots), jnp.int32),
            pltpu.VMEM(table, jnp.int32),
            pltpu.SMEM(table, jnp.int32),
            pltpu.SemaphoreType.DMA((STOPS, team_n, chunks)),
            pltpu.SemaphoreType.DMA((sends(team_n, chunks),)),
            pltpu.SemaphoreType.DMA((5,)),
        ],
        compiler_params=pltpu.CompilerParams(
            collective_id=0, has_side_effects=True, vmem_limit_bytes=60 * 1024 * 1024),
    )(row_count, column_of_slot.reshape(1, slots), blocks, probes)


def solution(mesh):
    spec = ("loop", "team")
    return jax.shard_map(
        functools.partial(local, mesh.shape["loop"], mesh.shape["team"]),
        mesh=mesh,
        in_specs=(P(spec, None, None), P(spec, None), P(spec), P(spec)),
        out_specs=P(spec, None),
        check_vma=False,
    )
```

time: 26.9 us -> 23.3 us (0.87)
  Pallas kernels: 25.1 us -> 21.5 us
    pallas_call x1, Pallas kernels: 25.1 us -> 21.5 us  [local(): pl.pallas_call(functools.partial(kernel, geo), out_shape=jax.ShapeDtypeSt...]
where the time goes in v3:
time: 23.3 us; the launch traced here: 23.1 us
  Pallas kernels  21.5 us (92%)
  local copies, waits for them, and re-layouts  1.57 us (7%)
    pallas_call x1, Pallas kernels, local(): pl.pallas_call(functools.partial(kernel, geo), out_shape=jax.ShapeDtypeSt...  21.5 us
    unnamed x1, local copies, waits for them, and re-layouts  1.57 us

profile of v3, /device:TPU:0, one launch (start us, length us, event | category | flops | bytes accessed | tf_op | source)
XLA Modules:
  0.0 23.1 jit_solution(12630334647898122345)
XLA Ops:
  0.0 21.5 %shard_map.46 = f32[256,128]{1,0:T(8,128)} custom-call(s32[2]{0:T(128)} %counts_hbm.1, s32[1,128]{1,0:T(1,128)} %bitcast.1, bf16[128,128,128]{2,1,0:T(8,128)(2,1)} %blocks_ref.1, bf16[1024,128]{1,0:T(8,128)(2,1)} %probes_ref.1), custom_call_target="tpu_custom_call" | custom-call | tf_op jit(solution)/shard_map/pallas_call | solution.py:211
  21.5 1.6 %copy.6 = f32[256,128]{1,0:T(8,128)} copy(f32[256,128]{1,0:T(8,128)} %shard_map.46) | data formatting | bytes 262144

commit v4 on v3

--- a/solution.py
+++ b/solution.py
@@ -19,8 +19,8 @@
     return x & (n - 1) if n & (n - 1) == 0 else lax.rem(x, n)
 
 
-def kernel(geo, counts_hbm, cols_hbm, blocks_ref, probes_ref, out_ref,
-           blk, win, counts_ref, cols_ref, inv_v, inv_s, recv, send, loc):
+def kernel(geo, meta_ref, blocks_ref, probes_ref, out_ref,
+           blk, win, inv_v, inv_s, recv, send, loc):
     loop_n, team_n, chunks, early, rows_here, slots, edge, tps = geo
     chunk = tps * edge // chunks
     per_piece = team_n * tps
@@ -35,13 +35,9 @@
         return {"loop": lax.rem(t + dt + loop_n, loop_n), "team": lax.rem(m + dm + team_n, team_n)}
 
     copies = [
-        pltpu.make_async_copy(counts_hbm, counts_ref, loc.at[0]),
-        pltpu.make_async_copy(cols_hbm, cols_ref, loc.at[1]),
-        pltpu.make_async_copy(probes_ref, win.at[0, 0], loc.at[2]),
-        pltpu.make_async_copy(blocks_ref, blk.at[pl.ds(0, slots)], loc.at[3]),
+        pltpu.make_async_copy(probes_ref, win.at[0, 0], loc.at[0]),
+        pltpu.make_async_copy(blocks_ref, blk.at[pl.ds(0, slots)], loc.at[1]),
     ]
-    for copy in copies:
-        copy.start()
 
     barrier = pltpu.get_barrier_semaphore()
 
@@ -54,17 +50,18 @@
         greet(0, d)
     greet(1 - 2 * core, 0)
 
-    copies[0].wait()
-    copies[1].wait()
-    col = cols_ref[...]
+    for copy in copies:
+        copy.start()
+
+    col = meta_ref[:, :slots]
     within = rem(col, per_piece)
     stop = rem(t - div(col, per_piece) + loop_n, loop_n)
     member = rem(m - div(within, tps) + team_n, team_n)
     key = (stop * team_n + member) * tps + rem(within, tps)
     number = lax.broadcasted_iota(jnp.int32, key.shape, 1)
-    end = jnp.int32(0)
+    end = jnp.zeros((1, 1), jnp.int32)
     for r in range(rows_here):
-        end = end + counts_ref[r]
+        end = end + meta_ref[:, slots + r:slots + r + 1]
         key = key + jnp.where(number >= end, span, 0)
     key = jnp.where(number < end, key, -1)
     entries = inv_v.shape[1]
@@ -72,7 +69,7 @@
     hit = keys == lax.broadcasted_iota(jnp.int32, (slots, entries), 1)
     owner = jnp.where(hit, lax.broadcasted_iota(jnp.int32, (slots, entries), 0), slots)
     inv_v[...] = jnp.min(owner, axis=0, keepdims=True)
-    inv_copy = pltpu.make_async_copy(inv_v, inv_s, loc.at[4])
+    inv_copy = pltpu.make_async_copy(inv_v, inv_s, loc.at[2])
     inv_copy.start()
     blk[slots] = jnp.zeros(blk.shape[1:], blk.dtype)
 
@@ -108,6 +105,10 @@
     out3 = jnp.where(odd == 1, odd3, even3)
     in2 = jnp.where(odd == 1, even2, odd2)
     in3 = out3
+    out2 = jnp.where(t + 2 >= loop_n, 0, out2)
+    out3 = jnp.where((t + 3 >= loop_n) & (odd == 1), 0, out3)
+    in2 = jnp.where(t < 2, 0, in2)
+    in3 = jnp.where((t < 3) & (odd == 1), 0, in3)
 
     for c in range(chunks):
         own = probes_ref.at[rows(c)]
@@ -117,8 +118,8 @@
             push(own, 0, d, c, at(0, d))
 
     inv_copy.wait()
-    copies[2].wait()
-    copies[3].wait()
+    for copy in copies:
+        copy.wait()
     step = 2 if tps % 2 == 0 else 1
 
     def compute(k, d):
@@ -208,12 +209,12 @@
     geo = (loop_n, team_n, chunks, early, rows_here, slots, edge, tps)
     entries = rows_here * STOPS * team_n * tps
     table = (1, -(-entries // LANES) * LANES)
+    meta = jnp.concatenate([column_of_slot, row_count]).reshape(1, slots + rows_here)
     return pl.pallas_call(
         functools.partial(kernel, geo),
         out_shape=jax.ShapeDtypeStruct((rows_here * edge, width), jnp.float32),
         in_specs=[
-            pl.BlockSpec(memory_space=pltpu.HBM),
-            pl.BlockSpec(memory_space=pltpu.HBM),
+            pl.BlockSpec(memory_space=pltpu.VMEM),
             pl.BlockSpec(memory_space=pltpu.HBM),
             pl.BlockSpec(memory_space=pltpu.HBM),
         ],
@@ -221,17 +222,15 @@
         scratch_shapes=[
             pltpu.VMEM((slots + 1, edge, edge), blocks.dtype),
             pltpu.VMEM((STOPS, team_n, tps * edge, width), probes.dtype),
-            pltpu.SMEM(row_count.shape, jnp.int32),
-            pltpu.VMEM((1, slots), jnp.int32),
             pltpu.VMEM(table, jnp.int32),
             pltpu.SMEM(table, jnp.int32),
             pltpu.SemaphoreType.DMA((STOPS, team_n, chunks)),
             pltpu.SemaphoreType.DMA((sends(team_n, chunks),)),
-            pltpu.SemaphoreType.DMA((5,)),
+            pltpu.SemaphoreType.DMA((3,)),
         ],
         compiler_params=pltpu.CompilerParams(
-            collective_id=0, has_side_effects=True, vmem_limit_bytes=60 * 1024 * 1024),
-    )(row_count, column_of_slot.reshape(1, slots), blocks, probes)
+            collective_id=0, has_side_effects=True, vmem_limit_bytes=55000 * 1024),
+    )(meta, blocks, probes)
 
 
 def solution(mesh):

time: 23.3 us -> 21.7 us (0.931)
  Pallas kernels: 21.5 us -> 20.2 us
  local copies, waits for them, and re-layouts: 1.57 us -> 0.66 us
  other arithmetic: 0 us -> 0.68 us
    pallas_call x1, Pallas kernels: 21.5 us -> 20.2 us  [local(): pl.pallas_call(functools.partial(kernel, geo), out_shape=jax.ShapeDtypeSt...]
    unnamed x1, local copies, waits for them, and re-layouts: 1.57 us -> 0.66 us
    concatenate x0 -> x1, other arithmetic: none -> 0.68 us  [local(): jnp.concatenate([column_of_slot, row_count]).reshape(1, slots + rows_here)]
where the time goes in v4:
time: 21.7 us; the launch traced here: 21.6 us
  Pallas kernels  20.2 us (93%)
  other arithmetic  0.68 us (3%)
  local copies, waits for them, and re-layouts  0.66 us (3%)
    pallas_call x1, Pallas kernels, local(): pl.pallas_call(functools.partial(kernel, geo), out_shape=jax.ShapeDtypeSt...  20.2 us
    concatenate x1, other arithmetic, local(): jnp.concatenate([column_of_slot, row_count]).reshape(1, slots + rows_here)  0.68 us
    unnamed x1, local copies, waits for them, and re-layouts  0.66 us

profile of v4, /device:TPU:0, one launch (start us, length us, event | category | flops | bytes accessed | tf_op | source)
XLA Modules:
  0.0 21.6 jit_solution(7011294655282486487)
XLA Ops:
  0.0 0.7 %pad_add_fusion = s32[130]{0:T(256)S(1)} fusion(s32[2]{0:T(128)} %param.6, s32[128]{0:T(128)} %param.7), kind=kLoop, calls=%fused_computation | loop fusion | flops 130 | bytes 1040 | tf_op jit(solution)/shard_map/concatenate | solution.py:212
  0.7 20.2 %shard_map.46 = f32[256,128]{1,0:T(8,128)S(1)} custom-call(s32[1,130]{1,0:T(1,128)S(1)} %bitcast.1, bf16[128,128,128]{2,1,0:T(8,128)(2,1)} %blocks_ref.1, bf16[1024,128]{1,0:T(8,128)(2,1)} %probes_ref.1), custom_call_target="tpu_custom_call" | custom-call | tf_op jit(solution)/shard_map/pallas_call | solution.py:213
  20.9 0.7 %copy.6 = f32[256,128]{1,0:T(8,128)} copy(f32[256,128]{1,0:T(8,128)S(1)} %shard_map.46) | data formatting | bytes 262144

commit v5 on v4

--- a/solution.py
+++ b/solution.py
@@ -45,7 +45,7 @@
         pl.semaphore_signal(barrier, inc=1, device_id=at(dt, dm), device_id_type=pl.DeviceIdType.MESH)
 
     pl.when(lower)(lambda: greet(-3, 0))
-    greet(-2, 0)
+    greet(jnp.where(t == 1, 1, -2), 0)
     for d in range(1, team_n):
         greet(0, d)
     greet(1 - 2 * core, 0)
@@ -73,7 +73,7 @@
     inv_copy.start()
     blk[slots] = jnp.zeros(blk.shape[1:], blk.dtype)
 
-    pl.semaphore_wait(barrier, team_n + 1 + core)
+    pl.semaphore_wait(barrier, team_n + 1 + core + jnp.where(t == 2, 1, 0) - jnp.where(t == loop_n - 1, 1, 0))
 
     sent = []
 
@@ -112,7 +112,7 @@
 
     for c in range(chunks):
         own = probes_ref.at[rows(c)]
-        push(own, 2, 0, c, ahead)
+        push(own, 2, 0, c, ahead, t != loop_n - 1)
         push(own, 1 + 2 * core, 0, c, across)
         for d in range(1, team_n):
             push(own, 0, d, c, at(0, d))
@@ -159,6 +159,7 @@
         @pl.when(lower)
         def _():
             arrive(3, 0, c)
+        push(win.at[3, 0, rows(c)], 2, 0, c, at(-1, 0), t == 2)
         for d in range(1, team_n):
             push(win.at[3, 0, rows(c)], 3, d, c, at(0, d), lower & ~first(c, in3))
 
@@ -196,7 +197,7 @@
 
 def sends(team_n, chunks):
     mates = team_n - 1
-    return chunks * (2 + mates + 2 * mates + mates + 1 + mates + mates)
+    return chunks * (2 + mates + 2 * mates + mates + 1 + mates + mates + 1)
 
 
 def local(loop_n, team_n, blocks, probes, row_count, column_of_slot):

time: 21.7 us -> 23.1 us (1.065)
  Pallas kernels: 20.2 us -> 21.6 us
    pallas_call x1, Pallas kernels: 20.2 us -> 21.6 us  [local(): pl.pallas_call(functools.partial(kernel, geo), out_shape=jax.ShapeDtypeSt...]
where the time goes in v5:
time: 23.1 us; the launch traced here: 22.9 us
  Pallas kernels  21.6 us (94%)
  other arithmetic  0.68 us (3%)
  local copies, waits for them, and re-layouts  0.66 us (3%)
    pallas_call x1, Pallas kernels, local(): pl.pallas_call(functools.partial(kernel, geo), out_shape=jax.ShapeDtypeSt...  21.6 us
    concatenate x1, other arithmetic, local(): jnp.concatenate([column_of_slot, row_count]).reshape(1, slots + rows_here)  0.68 us
    unnamed x1, local copies, waits for them, and re-layouts  0.66 us

profile of v5, /device:TPU:0, one launch (start us, length us, event | category | flops | bytes accessed | tf_op | source)
XLA Modules:
  0.0 22.9 jit_solution(15248108578566797815)
XLA Ops:
  0.0 0.7 %pad_add_fusion = s32[130]{0:T(256)S(1)} fusion(s32[2]{0:T(128)} %param.6, s32[128]{0:T(128)} %param.7), kind=kLoop, calls=%fused_computation | loop fusion | flops 130 | bytes 1040 | tf_op jit(solution)/shard_map/concatenate | solution.py:213
  0.7 21.6 %shard_map.46 = f32[256,128]{1,0:T(8,128)S(1)} custom-call(s32[1,130]{1,0:T(1,128)S(1)} %bitcast.1, bf16[128,128,128]{2,1,0:T(8,128)(2,1)} %blocks_ref.1, bf16[1024,128]{1,0:T(8,128)(2,1)} %probes_ref.1), custom_call_target="tpu_custom_call" | custom-call | tf_op jit(solution)/shard_map/pallas_call | solution.py:214
  22.3 0.7 %copy.6 = f32[256,128]{1,0:T(8,128)} copy(f32[256,128]{1,0:T(8,128)S(1)} %shard_map.46) | data formatting | bytes 262144
